TPU v7x, 256 devices: a whole 4x4x8 slice. The times are simulated.
256 devices in a mesh: ctx: 32 (over y, z), head: 8 (over x, core).
Axes of the slice: x: 4, y: 4, z: 8, core: 2. Of those that a mesh axis runs over, the one named last changes fastest.
Arguments:
- queries: bfloat16 [16384, 2048], P('ctx', 'head'), may hold values from -4.5 to 4.5
- keys: bfloat16 [16384, 1024], P('ctx', 'head'), may hold values from -4.5 to 4.5
- values: bfloat16 [16384, 1024], P('ctx', 'head'), may hold values from -4.5 to 4.5
- offsets: int32 [32], P('ctx'), may hold values from 0 to 512, as said below
- gate_logits: float32 [16], P('head'), may hold values from -2 to 2
- out_weight: bfloat16 [2048, 2048], P('head'), may hold values from -0.125 to 0.125
- grad_mixed: bfloat16 [16384, 2048], P('ctx', 'head'), may hold values from -6 to 6
Outputs:
- mixed: bfloat16 [16384, 2048], P('ctx', 'head')
- grad_queries: float32 [16384, 2048], P('ctx', 'head')
- grad_keys: float32 [16384, 1024], P('ctx', 'head')
- grad_values: float32 [16384, 1024], P('ctx', 'head')
- grad_weight: float32 [2048, 2048], P('head', 'ctx')
- grad_gates: float32 [16], P('head')
Inputs may be any that keep to these rules, and one draw needn't show every extreme that they name: `offsets`: entry s is 512 where segment s continues the document of the segment before it, else the position within segment s at which a new document begins.
All inputs are finite; a program needn't handle non-finite values.
Results may differ from a plain program's by a relative error of at most 0.0064.
Values may be sent and summed in bfloat16 or wider, within the bound.
No kernel may reach another device: no remote copies, remote signals or barrier semaphores. Data moves between devices by JAX's collectives and lax.ppermute only.
A program may use at most 64 MiB of HBM per device.

v0:
```python
import jax
import jax.numpy as jnp
from jax import lax
from jax.sharding import Mesh
from jax.sharding import PartitionSpec as P

HEAD_DIM = 128
SEG = 512
CTX = ("ctx_0", "ctx_1")
HEAD = ("head_0", "head_1")
highest = lax.Precision.HIGHEST


def neutral_like(value, identity):
    return jax.tree.map(
        lambda a, e: jnp.broadcast_to(jnp.asarray(e, a.dtype), a.shape), value, identity
    )


def collected_together(value, axis):
    leaves = jax.tree.leaves(value)
    order = sorted(range(len(leaves)), key=lambda k: -leaves[k].size)
    width = (1, *leaves[order[0]].shape)[-1]
    lines = [
        jnp.pad(leaves[k].reshape(-1), (0, -leaves[k].size % width)).reshape(-1, width)
        for k in order
    ]
    both, at, found = (lax.all_gather(jnp.concatenate(lines), axis), 0, {})
    for k, line in zip(order, lines):
        slab = both[:, at : at + len(line)].reshape(len(both), -1)
        found[k] = slab[:, : leaves[k].size].reshape(-1, *leaves[k].shape)
        at += len(line)
    numbers = iter(range(len(leaves)))
    return jax.tree.map(lambda _: found[next(numbers)], value)


def entering(value, axes, combine, identity):
    before = start = neutral_like(value, identity)
    running = value
    for axis in reversed(axes):
        size, index = (lax.axis_size(axis), lax.axis_index(axis))
        pieces = collected_together(running, axis)
        inside, running = (start, start)
        for k in range(size):
            passed = k < index
            running = combine(running, jax.tree.map(lambda part: part[k], pieces))
            inside = jax.tree.map(lambda new, old: jnp.where(passed, new, old), running, inside)
        before = combine(inside, before)
    return before


def piece_ends(length, count):
    unit = 8 if length >= 8 * count else 1
    return [length // unit * k // count * unit for k in range(1, count)]


def gather_in_order(value, axes, order):
    parts = value[None]
    for k in order:
        parts = lax.all_gather(parts, axes[k], axis=0, tiled=True)
    current = [lax.axis_size(axes[k]) for k in reversed(order)]
    parts = parts.reshape(*current, *value.shape)
    turned = sorted(range(len(order)), key=lambda place: order[len(order) - 1 - place])
    return parts.transpose(*turned, *range(len(order), parts.ndim)).reshape(-1, *value.shape)


def laid_out(parts, dim):
    dims = list(parts.shape[1:])
    dims[dim] *= parts.shape[0]
    return jnp.moveaxis(parts, 0, dim).reshape(dims)


def spread_gather(value, axes, dim):
    numbers = list(range(len(axes)))[::-1]
    cut = value.shape.index(max(value.shape[:-1] or value.shape))
    edges = [0, *piece_ends(value.shape[cut], len(axes)), value.shape[cut]]
    outs = []
    for k, (start, end) in enumerate(zip(edges, edges[1:])):
        if end > start:
            slab = lax.slice_in_dim(value, start, end, axis=cut)
            outs.append(gather_in_order(slab, axes, numbers[k:] + numbers[:k]))
    return laid_out(jnp.concatenate(outs, axis=cut + 1), dim)


def copy_for_each(value, axis):
    copies = jnp.broadcast_to(value, (lax.axis_size(axis), *value.shape))
    return lax.all_to_all(copies, axis, split_axis=0, concat_axis=0, tiled=True)


def collect(value, axis, dim):
    return laid_out(copy_for_each(value, axis), dim)


def cut_along(value, dim, size):
    before, after = (value.shape[:dim], value.shape[dim + 1 :])
    return jnp.moveaxis(value.reshape(*before, size, -1, *after), dim, 0)


def sent_and_summed(value, axis, dim):
    parts = cut_along(value, dim, lax.axis_size(axis))
    arrived = lax.all_to_all(parts, axis, split_axis=0, concat_axis=0, tiled=True)
    return arrived.sum(axis=0)


def gathered_by_type(value, axis):
    leaves, found = (jax.tree.leaves(value), {})
    for leading, a in enumerate(leaves):
        if leading not in found:
            alike = [k for k, b in enumerate(leaves) if b.dtype == a.dtype]
            got = (
                collected_together([leaves[k] for k in alike], axis)
                if len(alike) > 1
                else [lax.all_gather(a, axis)]
            )
            for k, b in zip(alike, got):
                found[k] = b
    numbers = iter(range(len(leaves)))
    return jax.tree.map(lambda _: found[next(numbers)], value)


def entering_2(value, axes, combine, identity):
    before = start = neutral_like(value, identity)
    running = value
    for axis in reversed(axes):
        size, index = (lax.axis_size(axis), lax.axis_index(axis))
        pieces = gathered_by_type(running, axis)
        inside, running = (start, start)
        for k in reversed(range(size)):
            passed = k > index
            running = combine(running, jax.tree.map(lambda part: part[k], pieces))
            inside = jax.tree.map(lambda new, old: jnp.where(passed, new, old), running, inside)
        before = combine(inside, before)
    return before


def of_everyone(value, axis):
    return copy_for_each(value, axis).sum(axis=0)


def feature(inputs):
    return jnp.where(inputs > 0, inputs + 1.0, jnp.exp(jnp.minimum(inputs, 0.0)))


def feature_slope(inputs):
    return jnp.where(inputs > 0, 1.0, jnp.exp(jnp.minimum(inputs, 0.0)))


def compose(earlier, later):
    return (
        later[2][:, None, None] * earlier[0] + later[0],
        later[2][:, None] * earlier[1] + later[1],
        earlier[2] * later[2],
    )


def segment_element(memory, totals, factor, segment):
    return (memory[segment], totals[segment], factor)


def body(queries, keys, values, offsets, gate_logits, out_weight, grad_mixed):
    tokens = queries.shape[0]
    head_count = queries.shape[1] // HEAD_DIM
    groups = keys.shape[1] // HEAD_DIM
    repeat = head_count // groups
    segments = tokens // SEG
    score_scale = HEAD_DIM ** (-0.5)
    query_blocks = queries.reshape(segments, SEG, groups, repeat, HEAD_DIM)
    key_blocks = keys.reshape(segments, SEG, groups, HEAD_DIM)
    value_blocks = values.reshape(segments, SEG, groups, HEAD_DIM)
    query_float = query_blocks.astype(jnp.float32)
    key_float = key_blocks.astype(jnp.float32)
    value_float = value_blocks.astype(jnp.float32)
    query_feat = feature(query_float)
    key_feat = feature(key_float)
    position = jnp.arange(SEG)
    retain = (position[None, :] < offsets[:, None]).astype(jnp.float32)
    start_cut = jnp.where(offsets == SEG, 0, offsets)
    counted = (position[None, :] >= start_cut[:, None]).astype(jnp.float32)
    carry_factor = (offsets == SEG).astype(jnp.float32)
    counted_feat = key_feat * counted[:, :, None, None]
    delta_memory = jnp.einsum("sjgd,sjge->sgde", counted_feat, value_float, precision=highest)
    delta_totals = jnp.sum(counted_feat, axis=1)
    identity = (
        jnp.zeros((groups, HEAD_DIM, HEAD_DIM), jnp.float32),
        jnp.zeros((groups, HEAD_DIM), jnp.float32),
        jnp.ones((1,), jnp.float32),
    )
    device_element = identity
    segment = 0
    device_element = compose(
        device_element, segment_element(delta_memory, delta_totals, carry_factor, segment)
    )
    incoming = entering(device_element, CTX, compose, identity)
    running = incoming
    segment = 0
    memory_list = [running[0]]
    totals_list = [running[1]]
    memory_in = jnp.stack(memory_list)
    totals_in = jnp.stack(totals_list)
    retained_feat = query_feat * retain[:, :, None, None, None]
    numerator = jnp.einsum("sigrd,sgde->sigre", retained_feat, memory_in, precision=highest)
    denominator = 1.0 + jnp.einsum("sigrd,sgd->sigr", retained_feat, totals_in, precision=highest)
    recall = numerator / denominator[..., None]
    scores = (
        jnp.einsum(
            "sigrd,sjgd->sgrij", query_blocks, key_blocks, preferred_element_type=jnp.float32
        )
        * score_scale
    )
    later_doc = position[None, :] >= offsets[:, None]
    allowed = (position[None, None, :] <= position[None, :, None]) & (
        later_doc[:, :, None] == later_doc[:, None, :]
    )
    scores = jnp.where(allowed[:, None, None], scores, -1e30)
    scaled_exp = jnp.exp(scores - jnp.max(scores, axis=-1, keepdims=True))
    weights = scaled_exp / jnp.sum(scaled_exp, axis=-1, keepdims=True)
    weights_low = weights.astype(jnp.bfloat16)
    attend = jnp.einsum(
        "sgrij,sjgd->sigrd", weights_low, value_blocks, preferred_element_type=jnp.float32
    )
    sigmoid_gate = jax.nn.sigmoid(gate_logits).reshape(groups, repeat)
    mixing = sigmoid_gate[None, None, :, :, None]
    output = (mixing * recall + (1.0 - mixing) * attend).astype(jnp.bfloat16)
    out_flat = output.reshape(tokens, head_count * HEAD_DIM)
    gathered = spread_gather(out_flat, HEAD, 1)
    weight_cols = lax.all_to_all(out_weight, HEAD, split_axis=1, concat_axis=0, tiled=True)
    mixed = jnp.dot(gathered, weight_cols, preferred_element_type=jnp.float32).astype(jnp.bfloat16)
    cotangent = collect(grad_mixed, HEAD, 1)
    grad_output = lax.dot_general(
        cotangent, out_weight, (((1,), (1,)), ((), ())), preferred_element_type=jnp.float32
    ).astype(jnp.bfloat16)
    weight_terms = lax.dot_general(
        out_flat, cotangent, (((0,), (0,)), ((), ())), preferred_element_type=jnp.float32
    )
    grad_weight = sent_and_summed(weight_terms, CTX, 1)
    grad_blocks = grad_output.reshape(segments, SEG, groups, repeat, HEAD_DIM)
    grad_float = grad_blocks.astype(jnp.float32)
    gate_slope = sigmoid_gate * (1.0 - sigmoid_gate)
    gate_terms = (jnp.sum(grad_float * (recall - attend), axis=(0, 1, 4)) * gate_slope).reshape(
        head_count
    )
    grad_recall = mixing * grad_float
    complement = (1.0 - sigmoid_gate)[None, :, :, None, None]
    grad_probs = complement * jnp.einsum(
        "sigrd,sjgd->sgrij", grad_blocks, value_blocks, preferred_element_type=jnp.float32
    )
    grad_scores = (
        weights * (grad_probs - jnp.sum(grad_probs * weights, axis=-1, keepdims=True)) * score_scale
    )
    grad_low = grad_scores.astype(jnp.bfloat16)
    grad_query = jnp.einsum(
        "sgrij,sjgd->sigrd", grad_low, key_blocks, preferred_element_type=jnp.float32
    )
    grad_key = jnp.einsum(
        "sgrij,sigrd->sjgd", grad_low, query_blocks, preferred_element_type=jnp.float32
    )
    value_terms = jnp.einsum(
        "sgrij,sigrd->sjgrd", weights_low, grad_blocks, preferred_element_type=jnp.float32
    )
    grad_value = jnp.sum(value_terms * (1.0 - sigmoid_gate)[None, None, :, :, None], axis=3)
    grad_numer = grad_recall / denominator[..., None]
    grad_denom = -jnp.sum(grad_recall * numerator, axis=-1) / (denominator * denominator)
    grad_feat = retain[:, :, None, None, None] * (
        jnp.einsum("sigre,sgde->sigrd", grad_numer, memory_in, precision=highest)
        + grad_denom[..., None] * totals_in[:, None, :, None, :]
    )
    grad_memory = jnp.einsum("sigrd,sigre->sgde", retained_feat, grad_numer, precision=highest)
    grad_totals = jnp.einsum("sigr,sigrd->sgd", grad_denom, retained_feat, precision=highest)
    grad_queries = (grad_query + grad_feat * feature_slope(query_float)).reshape(
        tokens, head_count * HEAD_DIM
    )
    device_grad = identity
    for segment in reversed(range(segments)):
        device_grad = compose(
            device_grad, segment_element(grad_memory, grad_totals, carry_factor, segment)
        )
    flowing = entering_2(device_grad, CTX, compose, identity)
    running = flowing
    flow_list = []
    flow_totals_list = []
    for segment in reversed(range(segments)):
        flow_list.append(running[0])
        flow_totals_list.append(running[1])
        running = compose(running, segment_element(grad_memory, grad_totals, carry_factor, segment))
    flow_memory = jnp.stack(flow_list[::-1])
    flow_totals = jnp.stack(flow_totals_list[::-1])
    counted_wide = counted[:, :, None, None]
    grad_key_feat = counted_wide * (
        jnp.einsum("sjge,sgde->sjgd", value_float, flow_memory, precision=highest)
        + flow_totals[:, None, :, :]
    )
    grad_keys = (grad_key + grad_key_feat * feature_slope(key_float)).reshape(
        tokens, groups * HEAD_DIM
    )
    grad_value_mem = counted_wide * jnp.einsum(
        "sjgd,sgde->sjge", key_feat, flow_memory, precision=highest
    )
    grad_values = (grad_value + grad_value_mem).reshape(tokens, groups * HEAD_DIM)
    grad_gates = of_everyone(gate_terms, CTX)
    return (mixed, grad_queries, grad_keys, grad_values, grad_weight, grad_gates)


def solution(mesh):
    torus = Mesh(mesh.devices.reshape(4, 8, 4, 2), ("ctx_0", "ctx_1", "head_0", "head_1"))
    in_specs = (
        P(CTX, HEAD),
        P(CTX, HEAD),
        P(CTX, HEAD),
        P(CTX),
        P(HEAD),
        P(HEAD, None),
        P(CTX, HEAD),
    )
    out_specs = (P(CTX, HEAD), P(CTX, HEAD), P(CTX, HEAD), P(CTX, HEAD), P(HEAD, CTX), P(HEAD))
    return jax.shard_map(body, mesh=torus, in_specs=in_specs, out_specs=out_specs, check_vma=False)
```

profile of v0, /device:TPU:8, one launch (start us, length us, event | category | flops | bytes accessed | tf_op | source)
XLA Modules:
  0.0 258.9 jit_solution(9639778417188686132)
XLA Ops:
  7.2 1.1 copy.129
  8.3 1.5 broadcast_in_dim.34
  9.8 4.4 %all-to-all-start.1 = ((bf16[8,512,256]{1,2,0:T(8,128)(2,1)}), bf16[8,512,256]{1,2,0:T(8,128)(2,1)S(1)}, u32[]{:S(2)}, u32[]{:S(2)}) async-start(bf16[8,512,256]{1,2,0:T(8,128)(2,1)} %broadcast_in_dim.34), calls=%async_computation.1 | async-start | bytes 4194304 | tf_op jit(solution)/shard_map/all_to_all | solution.py:87
  15.7 29.1 %all-gather.4 = f32[8,130,128]{2,1,0:T(8,128)S(1)} all-gather(f32[1,130,128]{2,1,0:T(8,128)S(1)} %fusion.61), channel_id=2, replica_groups=mesh['ctx_0'=4,'ctx_1'=8,'head_0'=4,'head_1'=2] {'ctx_1'}, dimensions={0}, use_global_device_ids=true | all-gather | bytes 599040 | tf_op jit(solution)/shard_map/all_gather | solution.py:28
  44.8 0.7 fusion.90
  46.1 4.9 %slice_add_fusion.16 = (f32[1,128,128]{2,1,0:T(8,128)S(1)}, f32[1,128,128]{2,1,0:T(8,128)}) fusion(f32[8,130,128]{2,1,0:T(8,128)S(1)} %all-gather.4, f32[]{:T(128)} %bitcast.23, f32[]{:T(128)} %bitcast.22, f32[]{:T(128)} %bitcast.25, f32[]{:T(128)} %bitcast.24, f32[]{:T(128)} %bitcast.29, f32[]{:T(128)} %bitcast.28, f32[]{:T(128)} %bitcast.27, f32[]{:T(128)} %bitcast.26), kind=kLoop, calls=%fused_computation.120 | loop fusion | flops 245760 | bytes 655392 | tf_op jit(solution)/shard_map/add | solution.py:150
  51.0 4.3 %slice_add_fusion.40 = (f32[1,1,128]{2,1,0:T(1,128)S(1)}, f32[1,1,128]{2,1,0:T(1,128)S(1)}, f32[1,1,128]{2,1,0:T(1,128)S(1)}) fusion(f32[8,130,128]{2,1,0:T(8,128)S(1)} %all-gather.4, f32[]{:T(128)} %bitcast.22, f32[]{:T(128)} %bitcast.23, f32[]{:T(128)} %bitcast.25, f32[]{:T(128)} %bitcast.24, f32[]{:T(128)} %bitcast.29, f32[]{:T(128)} %bitcast.28, ...), kind=kLoop, calls=%fused_computation.179 | loop fusion | flops 1920 | bytes 5664 | tf_op jit(solution)/shard_map/add | solution.py:151
  60.3 12.8 %all-gather.5 = f32[4,130,128]{2,1,0:T(8,128)S(1)} all-gather(f32[1,130,128]{2,1,0:T(8,128)S(1)} %maximum_bitcast_fusion.6), channel_id=3, replica_groups=mesh['ctx_0'=4,'ctx_1'=8,'head_0'=4,'head_1'=2] {'ctx_0'}, dimensions={0}, use_global_device_ids=true | all-gather | bytes 332800 | tf_op jit(solution)/shard_map/all_gather | solution.py:28
  73.8 1.1 fusion.30
  75.0 1.4 copy.186
  77.7 5.7 %bitcast_add_fusion.2 = (f32[128]{0:T(128)}, f32[1,1,128]{2,1,0:T(1,128)S(1)}, f32[1,1,128]{2,1,0:T(1,128)S(1)}) fusion(f32[1,1,128]{2,1,0:T(1,128)S(1)} %get-tuple-element.48, f32[1,1,128]{2,1,0:T(1,128)S(1)} %get-tuple-element.49, f32[1,1,128]{2,1,0:T(1,128)S(1)} %get-tuple-element.50, pred[]{:T(512)} %gt.71, pred[]{:T(512)} %gt.70, ...), kind=kLoop, calls=%fused_computation.190 | loop fusion | flops 3840 | bytes 7732 | tf_op jit(solution)/shard_map/add | solution.py:151
  83.3 1.8 fusion.76
  85.1 1.2 copy.147
  86.4 2.1 copy.134
  88.4 2.3 copy.127
  90.7 2.3 copy.128
  92.9 6.2 %fusion.70 = f32[128,128,1]{1,0,2:T(8,128)S(1)} fusion(f32[4,130,128]{2,1,0:T(8,128)} %copy-done.11, f32[1,128,128]{2,1,0:T(8,128)} %copy-done.15, f32[1,128,128]{2,1,0:T(8,128)} %get-tuple-element.47, f32[8,130,128]{2,1,0:T(8,128)} %copy-done.7, f32[]{:T(128)} %bitcast.38, f32[]{:T(128)} %bitcast.37, f32[]{:T(128)} %bitcast.36, f32[]{:T(128)} %bitcast.35, ...), kind=kLoop, calls=%fused_computation.116 | loop fusion | flops 524288 | bytes 852024 | tf_op jit(solution)/shard_map/reshape.106
  99.1 1.5 convolution_bitcast_fusion.5
  101.8 0.9 copy-done.1
  102.7 4.4 %all-to-all-start = ((bf16[256,8,256]{2,0,1:T(8,128)(2,1)}), bf16[256,8,256]{2,0,1:T(8,128)(2,1)}, u32[]{:S(2)}, u32[]{:S(2)}) async-start(bf16[256,8,256]{2,0,1:T(8,128)(2,1)} %copy.128), calls=%async_computation | async-start | bytes 2097152 | tf_op jit(solution)/shard_map/all_to_all | solution.py:226
  107.1 2.1 bitcast_divide_fusion
  109.3 0.7 multiply_reduce_fusion.1
  111.6 0.7 fusion.88
  112.4 2.1 convolution_bitcast_fusion
  114.4 8.7 %all-to-all-done = bf16[256,8,256]{2,0,1:T(8,128)(2,1)} async-done(((bf16[256,8,256]{2,0,1:T(8,128)(2,1)}), bf16[256,8,256]{2,0,1:T(8,128)(2,1)}, u32[]{:S(2)}, u32[]{:S(2)}) %all-to-all-start) | async-done | bytes 1048608 | tf_op jit(solution)/shard_map/all_to_all | solution.py:226
  123.8 7.8 %all-to-all-start.3 = ((f32[32,1,2]{2,1,0:T(1,128)}), f32[32,1,2]{2,1,0:T(1,128)S(1)}, u32[]{:S(2)}, u32[]{:S(2)}) async-start(f32[32,1,2]{2,1,0:T(1,128)} %broadcast_in_dim.35), calls=%async_computation.3 | async-start | bytes 32768 | tf_op jit(solution)/shard_map/all_to_all | solution.py:87
  131.6 26.8 %all-gather.6 = f32[8,130,128]{2,1,0:T(8,128)S(1)} all-gather(f32[1,130,128]{2,1,0:T(8,128)} %fusion.62), channel_id=4, replica_groups=mesh['ctx_0'=4,'ctx_1'=8,'head_0'=4,'head_1'=2] {'ctx_1'}, dimensions={0}, use_global_device_ids=true | all-gather | bytes 599040 | tf_op jit(solution)/shard_map/all_gather | solution.py:28
  158.4 1.7 copy.125
  160.0 8.8 %all-to-all-start.2 = ((f32[32,256,64]{1,2,0:T(8,128)}), f32[32,256,64]{1,2,0:T(8,128)}, u32[]{:S(2)}, u32[]{:S(2)}) async-start(f32[32,256,64]{1,2,0:T(8,128)} %convolution_bitcast_fusion), calls=%async_computation.2 | async-start | bytes 4194304 | tf_op jit(solution)/shard_map/all_to_all | solution.py:101
  168.9 13.9 %all_gather.42 = bf16[4,256,256]{2,1,0:T(8,128)(2,1)} all-gather(bf16[1,256,256]{2,1,0:T(8,128)(2,1)} %copy.125), channel_id=1, replica_groups=mesh['ctx_0'=4,'ctx_1'=8,'head_0'=4,'head_1'=2] {'head_0'}, dimensions={0}, use_global_device_ids=true | all-gather | bytes 655360 | tf_op jit(solution)/shard_map/all_gather | solution.py:60
  189.7 4.4 %slice_add_fusion.28 = (f32[1,1,128]{2,1,0:T(1,128)S(1)}, f32[1,1,128]{2,1,0:T(1,128)S(1)}, f32[1,1,128]{2,1,0:T(1,128)S(1)}) fusion(f32[8,130,128]{2,1,0:T(8,128)S(1)} %all-gather.6, f32[]{:T(128)} %bitcast.115, f32[]{:T(128)} %bitcast.116, f32[]{:T(128)} %bitcast.118, f32[]{:T(128)} %bitcast.117, f32[]{:T(128)} %bitcast.122, f32[]{:T(128)} %bitcast.121, ...), kind=kLoop, calls=%fused_computation.167 | loop fusion | flops 1920 | bytes 5664 | tf_op jit(solution)/shard_map/add | solution.py:151
  194.1 5.0 %slice_add_fusion.4 = (f32[1,128,128]{2,1,0:T(8,128)S(1)}, f32[1,128,128]{2,1,0:T(8,128)}) fusion(f32[8,130,128]{2,1,0:T(8,128)S(1)} %all-gather.6, f32[]{:T(128)} %bitcast.116, f32[]{:T(128)} %bitcast.115, f32[]{:T(128)} %bitcast.118, f32[]{:T(128)} %bitcast.117, f32[]{:T(128)} %bitcast.122, f32[]{:T(128)} %bitcast.121, f32[]{:T(128)} %bitcast.120, ...), kind=kLoop, calls=%fused_computation.104 | loop fusion | flops 245760 | bytes 655392 | tf_op jit(solution)/shard_map/add | solution.py:150
  199.8 12.5 %all-gather.7 = f32[4,130,128]{2,1,0:T(8,128)S(1)} all-gather(f32[1,130,128]{2,1,0:T(8,128)S(1)} %maximum_bitcast_fusion.7), channel_id=5, replica_groups=mesh['ctx_0'=4,'ctx_1'=8,'head_0'=4,'head_1'=2] {'ctx_0'}, dimensions={0}, use_global_device_ids=true | all-gather | bytes 332800 | tf_op jit(solution)/shard_map/all_gather | solution.py:28
  212.3 0.7 copy-done.10
  214.3 1.7 copy.124
  215.9 3.6 %all_gather.40 = bf16[2,256,256]{2,1,0:T(8,128)(2,1)} all-gather(bf16[1,256,256]{2,1,0:T(8,128)(2,1)} %copy.124), channel_id=1, replica_groups=mesh['ctx_0'=4,'ctx_1'=8,'head_0'=4,'head_1'=2] {'head_1'}, dimensions={0}, use_global_device_ids=true | all-gather | bytes 393216 | tf_op jit(solution)/shard_map/all_gather | solution.py:60
  219.6 1.7 multiply_reduce_fusion
  222.9 0.8 copy.141
  224.1 1.4 fusion.11
  225.6 2.1 copy.145
  227.6 6.1 %fusion.66 = f32[128,128]{1,0:T(8,128)S(1)} fusion(f32[4,130,128]{2,1,0:T(8,128)} %copy-done.10, f32[1,128,128]{2,1,0:T(8,128)} %copy-done.16, f32[1,128,128]{2,1,0:T(8,128)} %get-tuple-element.39, f32[8,130,128]{2,1,0:T(8,128)S(1)} %all-gather.6, f32[]{:T(128)} %bitcast.131, f32[]{:T(128)} %bitcast.130, f32[]{:T(128)} %bitcast.129, f32[]{:T(128)} %bitcast.128, ...), kind=kLoop, calls=%fused_computation.100 | loop fusion | flops 524288 | bytes 852024 | tf_op jit(solution)/shard_map/reshape.221
  233.7 2.0 fusion.23
  236.2 5.1 %bitcast_add_fusion.1 = f32[128]{0:T(128)S(1)} fusion(f32[1,1,128]{2,1,0:T(1,128)S(1)} %get-tuple-element.40, f32[1,1,128]{2,1,0:T(1,128)S(1)} %get-tuple-element.41, f32[1,1,128]{2,1,0:T(1,128)S(1)} %get-tuple-element.42, pred[]{:T(512)} %lt.62, pred[]{:T(512)} %lt.61, pred[]{:T(512)} %lt.60, pred[]{:T(512)} %lt.59, pred[]{:T(512)} %lt.58, pred[]{:T(512)} %lt.57, ...), kind=kLoop, calls=%fused_computation.189 | loop fusion | flops 3840 | bytes 6708 | tf_op jit(solution)/shard_map/add | solution.py:151
  241.3 1.0 fusion.19
  242.9 1.3 copy.126
  244.2 2.5 all-gather.11.cloned.1.call-done
  246.8 2.9 %fusion.13 = bf16[512,256]{1,0:T(8,128)(2,1)} fusion(bf16[8,256,256]{2,1,0:T(8,128)(2,1)S(1)} %bitcast.355, bf16[8,256,256]{2,1,0:T(8,128)(2,1)} %all-gather.11.cloned.1.call-done, bf16[256,8,256]{2,0,1:T(8,128)(2,1)} %all-to-all-done), kind=kOutput, calls=%fused_computation.25 | convolution fusion | flops 541196288 | bytes 3407872 | tf_op jit(solution)/shard_map/dot_general | solution.py:227
  249.7 2.3 reduce_sum.86
  (89 shorter events, 9.7 us)
Async XLA Ops:
  7.2 8.0 %copy-start = (bf16[512,128]{1,0:T(8,128)(2,1)S(1)}, bf16[512,128]{1,0:T(8,128)(2,1)}, u32[]{:S(2)}) copy-start(bf16[512,128]{1,0:T(8,128)(2,1)} %param.9) | copy-start | bytes 393220
  9.8 5.2 %copy-start.9 = (bf16[512,128]{1,0:T(8,128)(2,1)S(1)}, bf16[512,128]{1,0:T(8,128)(2,1)}, u32[]{:S(2)}) copy-start(bf16[512,128]{1,0:T(8,128)(2,1)} %param.8) | copy-start | bytes 393220
  9.8 92.9 %all-to-all-start.1 = ((bf16[8,512,256]{1,2,0:T(8,128)(2,1)}), bf16[8,512,256]{1,2,0:T(8,128)(2,1)S(1)}, u32[]{:S(2)}, u32[]{:S(2)}) async-start(bf16[8,512,256]{1,2,0:T(8,128)(2,1)} %broadcast_in_dim.34), calls=%async_computation.1 | async-start | bytes 4194304 | tf_op jit(solution)/shard_map/all_to_all | solution.py:87
  14.3 59.6 %copy-start.12 = (bf16[512,256]{1,0:T(8,128)(2,1)S(1)}, bf16[512,256]{1,0:T(8,128)(2,1)}, u32[]{:S(2)}) copy-start(bf16[512,256]{1,0:T(8,128)(2,1)} %param.7) | copy-start | bytes 786436
  44.8 6.2 %copy-start.7 = (f32[8,130,128]{2,1,0:T(8,128)}, f32[8,130,128]{2,1,0:T(8,128)S(1)}, u32[]{:S(2)}) copy-start(f32[8,130,128]{2,1,0:T(8,128)S(1)} %all-gather.4) | copy-start | bytes 1597444
  51.0 24.0 %copy-start.15 = (f32[1,128,128]{2,1,0:T(8,128)}, f32[1,128,128]{2,1,0:T(8,128)S(1)}, u32[]{:S(2)}) copy-start(f32[1,128,128]{2,1,0:T(8,128)S(1)} %get-tuple-element.46) | copy-start | bytes 196612
  73.1 0.7 copy-start.11
  75.0 24.1 %copy-start.5 = (f32[64,2,8,128]{3,2,1,0:T(8,128)}, f32[64,2,8,128]{3,2,1,0:T(8,128)S(1)}, u32[]{:S(2)}) copy-start(f32[64,2,8,128]{3,2,1,0:T(8,128)S(1)} %get-tuple-element.55) | copy-start | bytes 1572868
  92.9 7.8 %copy-start.13 = (bf16[512,256]{1,0:T(8,128)(2,1)S(1)}, bf16[512,256]{1,0:T(8,128)(2,1)}, u32[]{:S(2)}) copy-start(bf16[512,256]{1,0:T(8,128)(2,1)} %param.7) | copy-start | bytes 786436
  100.8 0.9 copy-start.23
  101.3 1.4 copy-start.1
  101.7 7.6 %copy-start.21 = (f32[2]{0:T(128)}, f32[2]{0:T(128)S(1)}, u32[]{:S(2)}) copy-start(f32[2]{0:T(128)S(1)} %get-tuple-element.51) | copy-start | bytes 28
  102.7 20.5 %all-to-all-start = ((bf16[256,8,256]{2,0,1:T(8,128)(2,1)}), bf16[256,8,256]{2,0,1:T(8,128)(2,1)}, u32[]{:S(2)}, u32[]{:S(2)}) async-start(bf16[256,8,256]{2,0,1:T(8,128)(2,1)} %copy.128), calls=%async_computation | async-start | bytes 2097152 | tf_op jit(solution)/shard_map/all_to_all | solution.py:226
  107.1 2.1 copy-start.2
  107.1 2.1 copy-start.17
  109.2 0.8 copy-start.18
  109.3 1.3 copy-start.6
  123.8 36.2 %all-to-all-start.3 = ((f32[32,1,2]{2,1,0:T(1,128)}), f32[32,1,2]{2,1,0:T(1,128)S(1)}, u32[]{:S(2)}, u32[]{:S(2)}) async-start(f32[32,1,2]{2,1,0:T(1,128)} %broadcast_in_dim.35), calls=%async_computation.3 | async-start | bytes 32768 | tf_op jit(solution)/shard_map/all_to_all | solution.py:87
  160.0 89.7 %all-to-all-start.2 = ((f32[32,256,64]{1,2,0:T(8,128)}), f32[32,256,64]{1,2,0:T(8,128)}, u32[]{:S(2)}, u32[]{:S(2)}) async-start(f32[32,256,64]{1,2,0:T(8,128)} %convolution_bitcast_fusion), calls=%async_computation.2 | async-start | bytes 4194304 | tf_op jit(solution)/shard_map/all_to_all | solution.py:101
  168.8 50.8 %copy-start.3 = (f32[1,1,2,512,512]{3,4,2,1,0:T(8,128)S(1)}, f32[1,1,2,512,512]{3,4,2,1,0:T(8,128)}, u32[]{:S(2)}) copy-start(f32[1,1,2,512,512]{3,4,2,1,0:T(8,128)} %copy-done.1) | copy-start | bytes 6291460
  168.8 74.1 %all-gather.13.cloned.1.call-start = ((), (), s32[]{:S(2)}) async-start(), calls=%async_computation.5 | async-start | bytes 1572864 | tf_op jit(solution)/shard_map/all_gather | solution.py:60
  182.8 64.0 %all-gather.11.cloned.1.call-start = ((), (), s32[]{:S(2)}) async-start(), calls=%async_computation.4 | async-start | bytes 1310720 | tf_op jit(solution)/shard_map/all_gather | solution.py:60
  199.1 0.6 copy-start.16
  212.3 0.7 copy-start.10
  219.6 1.7 copy-start.4
  219.6 1.7 copy-start.22
  221.4 1.0 copy-start.19
  222.9 1.2 copy-start.8
  222.9 1.2 copy-start.20
  225.6 10.2 %copy-start.14 = (bf16[512,256]{1,0:T(8,128)(2,1)S(1)}, bf16[512,256]{1,0:T(8,128)(2,1)}, u32[]{:S(2)}) copy-start(bf16[512,256]{1,0:T(8,128)(2,1)} %param.7) | copy-start | bytes 786436
Sparse Core Ops, SparseCore 0:
  182.9 13.7 all-gather.12
  219.7 26.9 all-gather.10
where the time goes:
time: 261 us; the launch traced here: 259 us
  blocking collectives  98.7 us (38%)
  other arithmetic  47.8 us (18%)
  between operations  29 us (11%)
  local copies, waits for them, and re-layouts  26.1 us (10%)
  starting transfers between devices  25.5 us (10%)
  matrix products  20.5 us (8%)
  waiting for transfers between devices  11.3 us (4%)
    all_gather x4, blocking collectives, collected_together(): both, at, found = (lax.all_gather(jnp.concatenate(lines), axis), 0, {})  81.2 us
    add x4, other arithmetic, compose(): later[2][:, None] * earlier[1] + later[1]  19.5 us
    all_gather x2, blocking collectives, gather_in_order(): parts = lax.all_gather(parts, axes[k], axis=0, tiled=True)  17.5 us
    another operation x3, other arithmetic  12.9 us
    all_to_all x2, starting transfers between devices, copy_for_each(): return lax.all_to_all(copies, axis, split_axis=0, concat_axis=0, tiled=True)  12.2 us
    add x2, other arithmetic, compose(): later[2][:, None, None] * earlier[0] + later[0]  9.96 us
    all_to_all x1, starting transfers between devices, sent_and_summed(): lax.all_to_all(parts, axis, split_axis=0, concat_axis=0, tiled=True)  8.76 us
    all_to_all x1, waiting for transfers between devices, body(): lax.all_to_all(out_weight, HEAD, split_axis=1, concat_axis=0, tiled=True)  8.74 us
  transfers between devices with their start and end apart: 6, of which 2 were waited for; matrix products, arithmetic and copies ran while one was open for 33% of the time, Pallas kernels for 0%

commit v1 on v0

--- a/solution.py
+++ b/solution.py
@@ -57,7 +57,9 @@
 def gather_in_order(value, axes, order):
     parts = value[None]
     for k in order:
-        parts = lax.all_gather(parts, axes[k], axis=0, tiled=True)
+        parts = jnp.concatenate(
+            lax.all_to_all(jnp.stack([parts] * lax.axis_size(axes[k])), axes[k], 0, 0), axis=0
+        )
     current = [lax.axis_size(axes[k]) for k in reversed(order)]
     parts = parts.reshape(*current, *value.shape)
     turned = sorted(range(len(order)), key=lambda place: order[len(order) - 1 - place])

time: 261 us -> 319 us (1.22)
  blocking collectives: 98.7 us -> 135 us
  waiting for transfers between devices: 11.3 us -> 30.3 us
  between operations: 29 us -> 16 us
  starting transfers between devices: 25.5 us -> 30.9 us
  matrix products: 20.5 us -> 24.5 us
  other arithmetic: 47.8 us -> 51.2 us
    all_gather x4, blocking collectives: 81.2 us -> 122 us  [collected_together(): both, at, found = (lax.all_gather(jnp.concatenate(lines), axis), 0, {})]
    all_gather x2 -> x0, blocking collectives: 17.5 us -> none  [gather_in_order(): parts = lax.all_gather(parts, axes[k], axis=0, tiled=True)]
    all_to_all x0 -> x2, waiting for transfers between devices: none -> 16.3 us  [gather_in_order(): lax.all_to_all(jnp.stack([parts] * lax.axis_size(axes[k])), axes[k], 0, 0)]
    all_to_all x0 -> x2, blocking collectives: none -> 12.5 us  [gather_in_order(): lax.all_to_all(jnp.stack([parts] * lax.axis_size(axes[k])), axes[k], 0, 0)]
    all_to_all x0 -> x2, starting transfers between devices: none -> 8.45 us  [gather_in_order(): lax.all_to_all(jnp.stack([parts] * lax.axis_size(axes[k])), axes[k], 0, 0)]
    another operation x0 -> x4, local copies, waits for them, and re-layouts: none -> 6.28 us  [gather_in_order(): jnp.stack([parts] * lax.axis_size(axes[k]))]
    all_to_all x2, waiting for transfers between devices: 0.01 us -> 6.24 us  [copy_for_each(): return lax.all_to_all(copies, axis, split_axis=0, concat_axis=0, tiled=True)]
    broadcast_in_dim x2 -> x0, local copies, waits for them, and re-layouts: 3.33 us -> none  [gather_in_order(): parts = value[None]]
  transfers between devices with their start and end apart: 6 -> 6, of which waited for: 2 -> 4; matrix products, arithmetic and copies ran while one was open for 33% -> 29% of each run, Pallas kernels for 0% -> 0%
where the time goes in v1:
time: 319 us; the launch traced here: 317 us
  blocking collectives  135 us (42%)
  other arithmetic  51.2 us (16%)
  starting transfers between devices  30.9 us (10%)
  waiting for transfers between devices  30.3 us (9%)
  local copies, waits for them, and re-layouts  29.2 us (9%)
  matrix products  24.5 us (8%)
  between operations  16 us (5%)
    all_gather x4, blocking collectives, collected_together(): both, at, found = (lax.all_gather(jnp.concatenate(lines), axis), 0, {})  122 us
    add x4, other arithmetic, compose(): later[2][:, None] * earlier[1] + later[1]  19.7 us
    all_to_all x2, waiting for transfers between devices, gather_in_order(): lax.all_to_all(jnp.stack([parts] * lax.axis_size(axes[k])), axes[k], 0, 0)  16.3 us
    all_to_all x2, blocking collectives, gather_in_order(): lax.all_to_all(jnp.stack([parts] * lax.axis_size(axes[k])), axes[k], 0, 0)  12.5 us
    all_to_all x2, starting transfers between devices, copy_for_each(): return lax.all_to_all(copies, axis, split_axis=0, concat_axis=0, tiled=True)  12.2 us
    another operation x3, other arithmetic  11.9 us
    add x2, other arithmetic, compose(): later[2][:, None, None] * earlier[0] + later[0]  10.2 us
    unnamed x57, local copies, waits for them, and re-layouts  8.64 us
  transfers between devices with their start and end apart: 6, of which 4 were waited for; matrix products, arithmetic and copies ran while one was open for 29% of the time, Pallas kernels for 0%

profile of v1, /device:TPU:8, one launch (start us, length us, event | category | flops | bytes accessed | tf_op | source)
XLA Modules:
  0.0 316.9 jit_solution(15532567984805036657)
XLA Ops:
  1.8 1.5 broadcast_in_dim.24
  3.3 4.4 %all-to-all-start.5 = ((bf16[8,512,256]{1,2,0:T(8,128)(2,1)}), bf16[8,512,256]{1,2,0:T(8,128)(2,1)S(1)}, u32[]{:S(2)}, u32[]{:S(2)}) async-start(bf16[8,512,256]{1,2,0:T(8,128)(2,1)} %broadcast_in_dim.24), calls=%async_computation.5 | async-start | bytes 4194304 | tf_op jit(solution)/shard_map/all_to_all | solution.py:89
  9.1 29.1 %all-gather.4 = f32[8,130,128]{2,1,0:T(8,128)S(1)} all-gather(f32[1,130,128]{2,1,0:T(8,128)S(1)} %fusion.61), channel_id=2, replica_groups=mesh['ctx_0'=4,'ctx_1'=8,'head_0'=4,'head_1'=2] {'ctx_1'}, dimensions={0}, use_global_device_ids=true | all-gather | bytes 599040 | tf_op jit(solution)/shard_map/all_gather | solution.py:28
  39.5 5.2 %slice_add_fusion.16 = (f32[1,128,128]{2,1,0:T(8,128)S(1)}, f32[1,128,128]{2,1,0:T(8,128)}) fusion(f32[8,130,128]{2,1,0:T(8,128)S(1)} %all-gather.4, f32[]{:T(128)} %bitcast.23, f32[]{:T(128)} %bitcast.22, f32[]{:T(128)} %bitcast.25, f32[]{:T(128)} %bitcast.24, f32[]{:T(128)} %bitcast.29, f32[]{:T(128)} %bitcast.28, f32[]{:T(128)} %bitcast.27, f32[]{:T(128)} %bitcast.26), kind=kLoop, calls=%fused_computation.122 | loop fusion | flops 245760 | bytes 655392 | tf_op jit(solution)/shard_map/add | solution.py:152
  44.7 4.5 %slice_add_fusion.40 = (f32[1,1,128]{2,1,0:T(1,128)S(1)}, f32[1,1,128]{2,1,0:T(1,128)S(1)}, f32[1,1,128]{2,1,0:T(1,128)S(1)}) fusion(f32[8,130,128]{2,1,0:T(8,128)S(1)} %all-gather.4, f32[]{:T(128)} %bitcast.22, f32[]{:T(128)} %bitcast.23, f32[]{:T(128)} %bitcast.25, f32[]{:T(128)} %bitcast.24, f32[]{:T(128)} %bitcast.29, f32[]{:T(128)} %bitcast.28, ...), kind=kLoop, calls=%fused_computation.181 | loop fusion | flops 1920 | bytes 5664 | tf_op jit(solution)/shard_map/add | solution.py:153
  54.5 12.8 %all-gather.5 = f32[4,130,128]{2,1,0:T(8,128)S(1)} all-gather(f32[1,130,128]{2,1,0:T(8,128)S(1)} %maximum_bitcast_fusion.6), channel_id=3, replica_groups=mesh['ctx_0'=4,'ctx_1'=8,'head_0'=4,'head_1'=2] {'ctx_0'}, dimensions={0}, use_global_device_ids=true | all-gather | bytes 332800 | tf_op jit(solution)/shard_map/all_gather | solution.py:28
  69.1 1.4 copy.186
  71.9 5.7 %bitcast_add_fusion.2 = (f32[128]{0:T(128)}, f32[1,1,128]{2,1,0:T(1,128)S(1)}, f32[1,1,128]{2,1,0:T(1,128)S(1)}) fusion(f32[1,1,128]{2,1,0:T(1,128)S(1)} %get-tuple-element.48, f32[1,1,128]{2,1,0:T(1,128)S(1)} %get-tuple-element.49, f32[1,1,128]{2,1,0:T(1,128)S(1)} %get-tuple-element.50, pred[]{:T(512)} %gt.71, pred[]{:T(512)} %gt.70, ...), kind=kLoop, calls=%fused_computation.192 | loop fusion | flops 3840 | bytes 7732 | tf_op jit(solution)/shard_map/add | solution.py:153
  77.6 1.8 fusion.76
  79.4 1.2 copy.147
  80.6 2.3 copy.127
  82.9 2.3 copy.128
  85.4 1.6 fusion.93
  88.4 5.1 %fusion.70 = f32[128,128,1]{1,0,2:T(8,128)S(1)} fusion(f32[4,130,128]{2,1,0:T(8,128)S(1)} %copy-done.12, f32[1,128,128]{2,1,0:T(8,128)S(1)} %copy-done.19, f32[1,128,128]{2,1,0:T(8,128)S(1)} %copy-done.22, f32[8,130,128]{2,1,0:T(8,128)S(1)} %copy-done.8, f32[]{:T(128)} %bitcast.38, f32[]{:T(128)} %bitcast.37, f32[]{:T(128)} %bitcast.36, f32[]{:T(128)} %bitcast.35, ...), kind=kLoop, calls=%fused_computation.118 | loop fusion | flops 524288 | bytes 852024 | tf_op jit(solution)/shard_map/reshape.105
  93.5 4.4 %all-to-all-start.4 = ((bf16[256,8,256]{2,0,1:T(8,128)(2,1)}), bf16[256,8,256]{2,0,1:T(8,128)(2,1)}, u32[]{:S(2)}, u32[]{:S(2)}) async-start(bf16[256,8,256]{2,0,1:T(8,128)(2,1)} %copy.128), calls=%async_computation.4 | async-start | bytes 2097152 | tf_op jit(solution)/shard_map/all_to_all | solution.py:228
  98.7 2.1 bitcast_divide_fusion
  102.9 1.7 copy.125
  104.6 1.7 pad_maximum_fusion.1
  106.3 7.7 %all-to-all-done.4 = bf16[256,8,256]{2,0,1:T(8,128)(2,1)} async-done(((bf16[256,8,256]{2,0,1:T(8,128)(2,1)}), bf16[256,8,256]{2,0,1:T(8,128)(2,1)}, u32[]{:S(2)}, u32[]{:S(2)}) %all-to-all-start.4) | async-done | bytes 1048608 | tf_op jit(solution)/shard_map/all_to_all | solution.py:228
  114.0 5.8 %all_to_all.52 = bf16[2,1,256,256]{2,3,1,0:T(8,128)(2,1)} all-to-all(bf16[2,1,256,256]{2,3,1,0:T(8,128)(2,1)} %pad_maximum_fusion.1), channel_id=1, replica_groups=mesh['ctx_0'=4,'ctx_1'=8,'head_0'=4,'head_1'=2] {'head_1'}, dimensions={0} | all-to-all | bytes 524288 | tf_op jit(solution)/shard_map/all_to_all | solution.py:61
  119.8 1.7 stack.17
  121.5 4.2 %all-to-all-start.2 = ((bf16[4,1,256,256]{3,2,1,0:T(8,128)(2,1)}), bf16[4,1,256,256]{3,2,1,0:T(8,128)(2,1)}, u32[]{:S(2)}, u32[]{:S(2)}) async-start(bf16[4,1,256,256]{3,2,1,0:T(8,128)(2,1)} %stack.17), calls=%async_computation.2 | async-start | bytes 1048576 | tf_op jit(solution)/shard_map/all_to_all | solution.py:61
  125.7 2.1 copy.134
  127.8 1.8 copy.124
  129.6 6.2 %all-to-all-done.2 = bf16[4,1,256,256]{3,2,1,0:T(8,128)(2,1)} async-done(((bf16[4,1,256,256]{3,2,1,0:T(8,128)(2,1)}), bf16[4,1,256,256]{3,2,1,0:T(8,128)(2,1)}, u32[]{:S(2)}, u32[]{:S(2)}) %all-to-all-start.2) | async-done | bytes 524320 | tf_op jit(solution)/shard_map/all_to_all | solution.py:61
  136.4 7.8 %all-to-all-start.7 = ((f32[32,1,2]{2,1,0:T(1,128)}), f32[32,1,2]{2,1,0:T(1,128)S(1)}, u32[]{:S(2)}, u32[]{:S(2)}) async-start(f32[32,1,2]{2,1,0:T(1,128)} %broadcast_in_dim.25), calls=%async_computation.7 | async-start | bytes 32768 | tf_op jit(solution)/shard_map/all_to_all | solution.py:89
  144.2 2.3 pad_maximum_fusion
  146.6 6.2 %all-to-all-done.7 = f32[32,1,2]{2,1,0:T(1,128)S(1)} async-done(((f32[32,1,2]{2,1,0:T(1,128)}), f32[32,1,2]{2,1,0:T(1,128)S(1)}, u32[]{:S(2)}, u32[]{:S(2)}) %all-to-all-start.7) | async-done | bytes 288 | tf_op jit(solution)/shard_map/all_to_all | solution.py:89
  152.8 6.7 %all_to_all.53 = bf16[2,4,256,256]{3,2,1,0:T(8,128)(2,1)} all-to-all(bf16[2,4,256,256]{3,2,1,0:T(8,128)(2,1)} %pad_maximum_fusion), channel_id=1, replica_groups=mesh['ctx_0'=4,'ctx_1'=8,'head_0'=4,'head_1'=2] {'head_1'}, dimensions={0} | all-to-all | bytes 2097152 | tf_op jit(solution)/shard_map/all_to_all | solution.py:61
  160.6 4.3 %all-to-all-start.1 = ((bf16[4,2,256,256]{3,2,1,0:T(8,128)(2,1)}), bf16[4,2,256,256]{3,2,1,0:T(8,128)(2,1)}, u32[]{:S(2)}, u32[]{:S(2)}) async-start(bf16[4,2,256,256]{3,2,1,0:T(8,128)(2,1)} %stack.16), calls=%async_computation.1 | async-start | bytes 2097152 | tf_op jit(solution)/shard_map/all_to_all | solution.py:61
  164.9 1.4 convolution_bitcast_fusion.10
  167.6 3.0 convolution_bitcast_fusion
  170.6 10.1 %all-to-all-done.1 = bf16[4,2,256,256]{3,2,1,0:T(8,128)(2,1)} async-done(((bf16[4,2,256,256]{3,2,1,0:T(8,128)(2,1)}), bf16[4,2,256,256]{3,2,1,0:T(8,128)(2,1)}, u32[]{:S(2)}, u32[]{:S(2)}) %all-to-all-start.1) | async-done | bytes 1048608 | tf_op jit(solution)/shard_map/all_to_all | solution.py:61
  180.6 5.8 %all-to-all-start.6 = ((f32[32,256,64]{1,2,0:T(8,128)}), f32[32,256,64]{1,2,0:T(8,128)}, u32[]{:S(2)}, u32[]{:S(2)}) async-start(f32[32,256,64]{1,2,0:T(8,128)} %convolution_bitcast_fusion), calls=%async_computation.6 | async-start | bytes 4194304 | tf_op jit(solution)/shard_map/all_to_all | solution.py:103
  186.5 68.0 %all-gather.6 = f32[8,130,128]{2,1,0:T(8,128)S(1)} all-gather(f32[1,130,128]{2,1,0:T(8,128)} %fusion.62), channel_id=4, replica_groups=mesh['ctx_0'=4,'ctx_1'=8,'head_0'=4,'head_1'=2] {'ctx_1'}, dimensions={0}, use_global_device_ids=true | all-gather | bytes 599040 | tf_op jit(solution)/shard_map/all_gather | solution.py:28
  261.4 4.4 %slice_add_fusion.28 = (f32[1,1,128]{2,1,0:T(1,128)S(1)}, f32[1,1,128]{2,1,0:T(1,128)S(1)}, f32[1,1,128]{2,1,0:T(1,128)S(1)}) fusion(f32[8,130,128]{2,1,0:T(8,128)S(1)} %all-gather.6, f32[]{:T(128)} %bitcast.117, f32[]{:T(128)} %bitcast.118, f32[]{:T(128)} %bitcast.120, f32[]{:T(128)} %bitcast.119, f32[]{:T(128)} %bitcast.124, f32[]{:T(128)} %bitcast.123, ...), kind=kLoop, calls=%fused_computation.169 | loop fusion | flops 1920 | bytes 5664 | tf_op jit(solution)/shard_map/add | solution.py:153
  265.7 5.0 %slice_add_fusion.4 = (f32[1,128,128]{2,1,0:T(8,128)S(1)}, f32[1,128,128]{2,1,0:T(8,128)}) fusion(f32[8,130,128]{2,1,0:T(8,128)S(1)} %all-gather.6, f32[]{:T(128)} %bitcast.118, f32[]{:T(128)} %bitcast.117, f32[]{:T(128)} %bitcast.120, f32[]{:T(128)} %bitcast.119, f32[]{:T(128)} %bitcast.124, f32[]{:T(128)} %bitcast.123, f32[]{:T(128)} %bitcast.122, ...), kind=kLoop, calls=%fused_computation.106 | loop fusion | flops 245760 | bytes 655392 | tf_op jit(solution)/shard_map/add | solution.py:152
  271.4 12.6 %all-gather.7 = f32[4,130,128]{2,1,0:T(8,128)S(1)} all-gather(f32[1,130,128]{2,1,0:T(8,128)S(1)} %maximum_bitcast_fusion.7), channel_id=5, replica_groups=mesh['ctx_0'=4,'ctx_1'=8,'head_0'=4,'head_1'=2] {'ctx_0'}, dimensions={0}, use_global_device_ids=true | all-gather | bytes 332800 | tf_op jit(solution)/shard_map/all_gather | solution.py:28
  285.9 2.2 fusion.12
  288.2 1.8 copy.141
  289.9 1.7 multiply_reduce_fusion
  292.7 1.5 fusion.11
  294.2 2.1 copy.145
  296.3 6.1 %fusion.66 = f32[128,128]{1,0:T(8,128)S(1)} fusion(f32[4,130,128]{2,1,0:T(8,128)} %copy-done.13, f32[1,128,128]{2,1,0:T(8,128)} %copy-done.20, f32[1,128,128]{2,1,0:T(8,128)} %get-tuple-element.39, f32[8,130,128]{2,1,0:T(8,128)S(1)} %all-gather.6, f32[]{:T(128)} %bitcast.133, f32[]{:T(128)} %bitcast.132, f32[]{:T(128)} %bitcast.131, f32[]{:T(128)} %bitcast.130, ...), kind=kLoop, calls=%fused_computation.102 | loop fusion | flops 524288 | bytes 852024 | tf_op jit(solution)/shard_map/reshape.222
  302.4 2.0 fusion.23
  304.8 5.1 %bitcast_add_fusion.1 = f32[128]{0:T(128)S(1)} fusion(f32[1,1,128]{2,1,0:T(1,128)S(1)} %get-tuple-element.40, f32[1,1,128]{2,1,0:T(1,128)S(1)} %get-tuple-element.41, f32[1,1,128]{2,1,0:T(1,128)S(1)} %get-tuple-element.42, pred[]{:T(512)} %lt.62, pred[]{:T(512)} %lt.61, pred[]{:T(512)} %lt.60, pred[]{:T(512)} %lt.59, pred[]{:T(512)} %lt.58, pred[]{:T(512)} %lt.57, ...), kind=kLoop, calls=%fused_computation.191 | loop fusion | flops 3840 | bytes 6708 | tf_op jit(solution)/shard_map/add | solution.py:153
  311.6 3.0 fusion.13
  314.5 2.3 reduce_sum.86
  (97 shorter events, 17.3 us)
Async XLA Ops:
  0.6 8.0 %copy-start = (bf16[512,128]{1,0:T(8,128)(2,1)S(1)}, bf16[512,128]{1,0:T(8,128)(2,1)}, u32[]{:S(2)}) copy-start(bf16[512,128]{1,0:T(8,128)(2,1)} %param.9) | copy-start | bytes 393220
  3.3 5.2 %copy-start.10 = (bf16[512,128]{1,0:T(8,128)(2,1)S(1)}, bf16[512,128]{1,0:T(8,128)(2,1)}, u32[]{:S(2)}) copy-start(bf16[512,128]{1,0:T(8,128)(2,1)} %param.8) | copy-start | bytes 393220
  3.3 90.3 %all-to-all-start.5 = ((bf16[8,512,256]{1,2,0:T(8,128)(2,1)}), bf16[8,512,256]{1,2,0:T(8,128)(2,1)S(1)}, u32[]{:S(2)}, u32[]{:S(2)}) async-start(bf16[8,512,256]{1,2,0:T(8,128)(2,1)} %broadcast_in_dim.24), calls=%async_computation.5 | async-start | bytes 4194304 | tf_op jit(solution)/shard_map/all_to_all | solution.py:89
  7.7 60.3 %copy-start.16 = (bf16[512,256]{1,0:T(8,128)(2,1)S(1)}, bf16[512,256]{1,0:T(8,128)(2,1)}, u32[]{:S(2)}) copy-start(bf16[512,256]{1,0:T(8,128)(2,1)} %param.7) | copy-start | bytes 786436
  38.2 6.5 %copy-start.7 = (f32[8,130,128]{2,1,0:T(8,128)}, f32[8,130,128]{2,1,0:T(8,128)S(1)}, u32[]{:S(2)}) copy-start(f32[8,130,128]{2,1,0:T(8,128)S(1)} %all-gather.4) | copy-start | bytes 1597444
  44.7 24.4 %copy-start.18 = (f32[1,128,128]{2,1,0:T(8,128)}, f32[1,128,128]{2,1,0:T(8,128)S(1)}, u32[]{:S(2)}) copy-start(f32[1,128,128]{2,1,0:T(8,128)S(1)} %get-tuple-element.46) | copy-start | bytes 196612
  67.3 0.7 copy-start.11
  69.1 28.8 %copy-start.5 = (f32[64,2,8,128]{3,2,1,0:T(8,128)}, f32[64,2,8,128]{3,2,1,0:T(8,128)S(1)}, u32[]{:S(2)}) copy-start(f32[64,2,8,128]{3,2,1,0:T(8,128)S(1)} %get-tuple-element.55) | copy-start | bytes 1572868
  85.4 2.0 copy-start.26
  85.4 3.0 copy-start.8
  85.4 3.0 copy-start.12
  85.4 3.0 copy-start.19
  85.4 3.0 copy-start.22
  87.0 1.3 copy-start.1
  87.4 13.4 %copy-start.24 = (f32[2]{0:T(128)}, f32[2]{0:T(128)S(1)}, u32[]{:S(2)}) copy-start(f32[2]{0:T(128)S(1)} %get-tuple-element.51) | copy-start | bytes 28
  93.5 20.5 %all-to-all-start.4 = ((bf16[256,8,256]{2,0,1:T(8,128)(2,1)}), bf16[256,8,256]{2,0,1:T(8,128)(2,1)}, u32[]{:S(2)}, u32[]{:S(2)}) async-start(bf16[256,8,256]{2,0,1:T(8,128)(2,1)} %copy.128), calls=%async_computation.4 | async-start | bytes 2097152 | tf_op jit(solution)/shard_map/all_to_all | solution.py:228
  98.6 2.1 copy-start.2
  100.7 0.7 copy-start.21
  101.5 0.7 copy-start.14
  121.5 14.3 %all-to-all-start.2 = ((bf16[4,1,256,256]{3,2,1,0:T(8,128)(2,1)}), bf16[4,1,256,256]{3,2,1,0:T(8,128)(2,1)}, u32[]{:S(2)}, u32[]{:S(2)}) async-start(bf16[4,1,256,256]{3,2,1,0:T(8,128)(2,1)} %stack.17), calls=%async_computation.2 | async-start | bytes 1048576 | tf_op jit(solution)/shard_map/all_to_all | solution.py:61
  136.4 16.3 %all-to-all-start.7 = ((f32[32,1,2]{2,1,0:T(1,128)}), f32[32,1,2]{2,1,0:T(1,128)S(1)}, u32[]{:S(2)}, u32[]{:S(2)}) async-start(f32[32,1,2]{2,1,0:T(1,128)} %broadcast_in_dim.25), calls=%async_computation.7 | async-start | bytes 32768 | tf_op jit(solution)/shard_map/all_to_all | solution.py:89
  152.8 6.7 %copy-start.15 = (bf16[2,256,256]{2,1,0:T(8,128)(2,1)S(1)}, bf16[2,256,256]{2,1,0:T(8,128)(2,1)}, u32[]{:S(2)}) copy-start(bf16[2,256,256]{2,1,0:T(8,128)(2,1)} %copy.124) | copy-start | bytes 786436
  160.6 20.0 %all-to-all-start.1 = ((bf16[4,2,256,256]{3,2,1,0:T(8,128)(2,1)}), bf16[4,2,256,256]{3,2,1,0:T(8,128)(2,1)}, u32[]{:S(2)}, u32[]{:S(2)}) async-start(bf16[4,2,256,256]{3,2,1,0:T(8,128)(2,1)} %stack.16), calls=%async_computation.1 | async-start | bytes 2097152 | tf_op jit(solution)/shard_map/all_to_all | solution.py:61
  170.6 115.4 %copy-start.3 = (f32[1,1,2,512,512]{3,4,2,1,0:T(8,128)S(1)}, f32[1,1,2,512,512]{3,4,2,1,0:T(8,128)}, u32[]{:S(2)}) copy-start(f32[1,1,2,512,512]{3,4,2,1,0:T(8,128)} %copy-done.1) | copy-start | bytes 6291460
  180.6 133.9 %all-to-all-start.6 = ((f32[32,256,64]{1,2,0:T(8,128)}), f32[32,256,64]{1,2,0:T(8,128)}, u32[]{:S(2)}, u32[]{:S(2)}) async-start(f32[32,256,64]{1,2,0:T(8,128)} %convolution_bitcast_fusion), calls=%async_computation.6 | async-start | bytes 4194304 | tf_op jit(solution)/shard_map/all_to_all | solution.py:103
  270.8 0.6 copy-start.20
  284.0 0.7 copy-start.13
  289.9 1.7 copy-start.4
  289.9 1.7 copy-start.25
  291.7 1.0 copy-start.9
  291.7 1.0 copy-start.23
  294.2 10.2 %copy-start.17 = (bf16[512,256]{1,0:T(8,128)(2,1)S(1)}, bf16[512,256]{1,0:T(8,128)(2,1)}, u32[]{:S(2)}) copy-start(bf16[512,256]{1,0:T(8,128)(2,1)} %param.7) | copy-start | bytes 786436
  296.3 15.2 %copy-start.6 = (bf16[2,4,256,256]{3,2,1,0:T(8,128)(2,1)S(1)}, bf16[2,4,256,256]{3,2,1,0:T(8,128)(2,1)}, u32[]{:S(2)}) copy-start(bf16[2,4,256,256]{3,2,1,0:T(8,128)(2,1)} %all_to_all.53) | copy-start | bytes 3145732
